TPU v7x, 32 devices: a whole 2x2x4 slice. The times are simulated.
32 devices in a mesh: grp: 2 (over y), pool: 4 (over z), head: 2 (over x), aux: 2 (over core).
Axes of the slice: x: 2, y: 2, z: 4, core: 2. Of those that a mesh axis runs over, the one named last changes fastest.
Arguments:
- hidden: bfloat16 [16, 8192], P('grp', ('pool', 'head', 'aux')), parts along dimension 0, may hold values from -0.59765625 to 0.59765625
- gain: float32 [8192], P(('pool', 'head', 'aux')), may hold values from 0.5 to 1.5
- queries: bfloat16 [16, 8192], P(('grp', 'pool'), 'aux'), parts along dimension 0, may hold values from -6 to 6
- new_key: bfloat16 [16, 1024], P(('grp', 'pool'), 'aux'), parts along dimension 0, may hold values from -6 to 6
- new_value: bfloat16 [16, 1024], P(('grp', 'pool'), 'aux'), parts along dimension 0, may hold values from -6 to 6
- cache_key: bfloat16 [16, 512, 1024], P(('grp', 'pool'), 'head', 'aux'), parts along dimension 0, may hold values from -6 to 6
- cache_value: bfloat16 [16, 512, 1024], P(('grp', 'pool'), 'head', 'aux'), parts along dimension 0, may hold values from -6 to 6
- lengths: int32 [16], P('grp'), parts along dimension 0, may hold values from 170 to 512, as said below
- slot_of: int32 [16], P('grp'), parts along dimension 0, may hold values from 0 to 7, as said below
- out_proj: bfloat16 [2, 4096, 8192], P('aux', 'head', 'pool'), may hold values from -0.09375 to 0.09375
- lm_head: bfloat16 [8192, 65536], P(None, ('pool', 'head', 'aux')), may hold values from -1 to 1
Outputs:
- logits: float32 [16, 65536], P('grp', ('pool', 'head', 'aux')), parts along dimension 0
- entropy: float32 [16], P('grp'), parts along dimension 0
There are 2 independent parts, one for each index of `grp`. A program takes and returns all parts, laid end to end along the dimension named above; an argument that names none is the same for every part. Nothing has to cross between parts.
Inputs may be any that keep to these rules, and one draw needn't show every extreme that they name: `lengths`: some request fills all 512 positions and some has exactly 170. `slot_of`: each slot holds exactly one request; the requests of one index of pool have their slots together on one index of pool.
All inputs are finite; a program needn't handle non-finite values.
Results may differ from a plain program's by a relative error of at most 0.02.
Values may be sent and summed in bfloat16 or wider, within the bound.
No kernel may reach another device: no remote copies, remote signals or barrier semaphores. Data moves between devices by JAX's collectives and lax.ppermute only.
A program may use at most 128 MiB of HBM per device.

v0:
```python
import math

import jax
import jax.numpy as jnp
from jax import lax
from jax.experimental import pallas as pl
from jax.experimental.pallas import tpu as pltpu
from jax.sharding import PartitionSpec as P

HD = 128


class Rounds:
    def __init__(self, lm_head):
        self.lm_head = lm_head
        self.resident = []

    def swap(self, x, axis, size, step):
        pairs = [(i, i ^ step) for i in range(size)]
        if axis == "aux" or len(self.resident) == WINDOWS:
            return lax.ppermute(x, axis, pairs)
        at = len(self.resident)
        y = lax.ppermute(x, axis, pairs)
        self.resident.append(fetch(self.lm_head, at))
        return y


def gather(rounds, x, axis, size, dim):
    place = lax.axis_index(axis)
    step = 1
    while step < size:
        y = rounds.swap(x, axis, size, step)
        upper = (place & step) != 0
        x = jnp.concatenate([jnp.where(upper, y, x), jnp.where(upper, x, y)], dim)
        step *= 2
    return x


VM = pl.BlockSpec(memory_space=pltpu.VMEM)
HB = pl.BlockSpec(memory_space=pl.ANY)
MIB = 1 << 20
WINDOWS = 8
PIECES = 16


def fetch(lm_head, piece):
    rows = lm_head.shape[0] // PIECES
    cuts = 4
    part = rows // cuts

    def body(src, dst, sem):
        copies = [
            pltpu.make_async_copy(
                src.at[pl.ds(piece * rows + i * part, part)],
                dst.at[pl.ds(i * part, part)],
                sem.at[i],
            )
            for i in range(cuts)
        ]
        for copy in copies:
            copy.start()
        for copy in copies:
            copy.wait()

    return pl.pallas_call(
        body,
        out_shape=pltpu.VMEM((rows, lm_head.shape[1]), lm_head.dtype),
        in_specs=[HB],
        out_specs=VM,
        scratch_shapes=[pltpu.SemaphoreType.DMA((cuts,))],
        cost_estimate=pl.CostEstimate(
            flops=0, bytes_accessed=rows * lm_head.shape[1] * 2, transcendentals=0
        ),
        compiler_params=pltpu.CompilerParams(vmem_limit_bytes=MIB),
    )(lm_head)


def join(*arrays):
    widths = [a.shape[1] for a in arrays]

    def body(*refs):
        at = 0
        for ref, width in zip(refs[:-1], widths):
            refs[-1][:, at : at + width] = ref[...]
            at += width

    return pl.pallas_call(
        body,
        out_shape=jax.ShapeDtypeStruct((arrays[0].shape[0], sum(widths)), arrays[0].dtype),
        in_specs=[VM] * len(arrays),
        out_specs=VM,
        compiler_params=pltpu.CompilerParams(vmem_limit_bytes=2 * MIB),
        name="join",
    )(*arrays)


def project(outputs, order, weight, hidden, place, gains):
    requests, width = outputs.shape[0], weight.shape[1]
    chunk = hidden.shape[1]
    f32, bf16 = jnp.float32, jnp.bfloat16

    def body(place_ref, out_ref, order_ref, w_ref, hid_ref, gain_ref, term_ref, msg_ref):
        rows = out_ref[...].astype(f32)
        pick = order_ref[...]
        sel = jnp.zeros_like(rows)
        for e in range(requests):
            sel = sel + pick[:, e : e + 1] * rows[e : e + 1, :]
        term = jnp.dot(sel.astype(bf16), w_ref[...], preferred_element_type=f32)
        tiled = jnp.concatenate([hid_ref[...].astype(f32)] * (width // chunk), 1)
        owner = lax.broadcasted_iota(jnp.int32, term.shape, 1) // chunk == place_ref[0]
        term = term + jnp.where(owner, tiled, 0.0)
        term_ref[...] = term
        msg_ref[:, :width] = term.astype(bf16)
        msg_ref[:, width:] = gain_ref[...]

    return pl.pallas_call(
        body,
        out_shape=(
            jax.ShapeDtypeStruct((requests, width), f32),
            jax.ShapeDtypeStruct((requests, width + gains.shape[1]), bf16),
        ),
        in_specs=[pl.BlockSpec(memory_space=pltpu.SMEM)] + [VM] * 5,
        out_specs=(VM, VM),
        cost_estimate=pl.CostEstimate(
            flops=2 * requests * weight.size, bytes_accessed=weight.size * 2, transcendentals=0
        ),
        compiler_params=pltpu.CompilerParams(vmem_limit_bytes=4 * MIB),
        name="project",
    )(place, outputs, order, weight, hidden, gains)


def score(x, resident, lm_head):
    requests, depth = x.shape
    width = lm_head.shape[1]
    held = len(resident)
    rows = depth // PIECES
    start = held * rows
    left = PIECES - held
    slots = min(3, left)
    f32, bf16 = jnp.float32, jnp.bfloat16

    def body(x_ref, *refs):
        kept = refs[:held]
        src, out_ref, sum_ref, buf, sem = refs[held:]

        def copy(i):
            return pltpu.make_async_copy(
                src.at[pl.ds(start + i * rows, rows)], buf.at[i % slots], sem.at[i % slots]
            )

        for i in range(slots):
            copy(i).start()

        def multiply(ref, piece, first=False):
            part = jnp.dot(
                x_ref[:, piece * rows : (piece + 1) * rows], ref[...], preferred_element_type=f32
            )
            out_ref[...] = part if first else out_ref[...] + part

        done = 0
        for i in range(held):
            multiply(kept[i], i, i == 0)
            while done < left and done * held < (i + 1) * left:
                copy(done).wait()
                multiply(buf.at[done % slots], held + done)
                if done + slots < left:
                    copy(done + slots).start()
                done += 1
        logits = out_ref[...]
        expd = jnp.exp(logits)
        total = jnp.sum(expd, axis=1, keepdims=True)
        moment = jnp.sum(expd * logits, axis=1, keepdims=True)
        lane = lax.broadcasted_iota(jnp.int32, (requests, 128), 1)
        sum_ref[...] = jnp.where(lane == 0, total, moment)

    return pl.pallas_call(
        body,
        out_shape=(
            jax.ShapeDtypeStruct((requests, width), f32),
            jax.ShapeDtypeStruct((requests, 128), f32),
        ),
        in_specs=[VM] * (1 + held) + [HB],
        out_specs=(VM, VM),
        scratch_shapes=[
            pltpu.VMEM((slots, rows, width), bf16),
            pltpu.SemaphoreType.DMA((slots,)),
        ],
        cost_estimate=pl.CostEstimate(
            flops=2 * requests * lm_head.size,
            bytes_accessed=left * rows * width * 2,
            transcendentals=requests * width,
        ),
        compiler_params=pltpu.CompilerParams(vmem_limit_bytes=slots * rows * width * 2 + 4 * MIB),
        name="score",
    )(x, *resident, lm_head)


def total_over(rounds, x, axes_sizes):
    for axis, size in axes_sizes:
        step = 1
        while step < size:
            x = x + rounds.swap(x, axis, size, step)
            step *= 2
    return x


def make_per_device(sizes):
    n_pool, n_head, n_aux = sizes["pool"], sizes["head"], sizes["aux"]

    def per_device(
        hidden,
        gain,
        queries,
        new_key,
        new_value,
        cache_key,
        cache_value,
        lengths,
        slot_of,
        out_proj,
        lm_head,
    ):
        f32, bf16 = jnp.float32, jnp.bfloat16
        slots_here, span = cache_key.shape[0], cache_key.shape[1]
        kv_here = cache_key.shape[2] // HD
        q_here = queries.shape[1] // HD
        group = q_here // kv_here
        requests = hidden.shape[0]
        scale = 1.0 / math.sqrt(HD)
        pool_place = lax.axis_index("pool")
        head_place = lax.axis_index("head")
        aux_place = lax.axis_index("aux")

        rounds = Rounds(lm_head)
        every = gather(rounds, join(queries, new_key, new_value), "pool", n_pool, 0)
        nq, nk = queries.shape[1], new_key.shape[1]

        slot_ids = pool_place * slots_here + jnp.arange(slots_here, dtype=jnp.int32)
        chosen = slot_of[None, :] == slot_ids[:, None]
        picked = jnp.dot(
            chosen.astype(bf16), every, preferred_element_type=f32
        ).astype(bf16)
        query_heads = picked[:, :nq].reshape(slots_here, kv_here, group, HD)
        key_own = picked[:, nq : nq + nk].reshape(slots_here, kv_here, 1, HD).astype(f32)
        value_own = picked[:, nq + nk :].reshape(slots_here, kv_here, 1, HD).astype(f32)
        length_slot = jnp.sum(jnp.where(chosen, lengths[None, :], 0), axis=1)
        keys = cache_key.reshape(slots_here, span, kv_here, HD)
        values = cache_value.reshape(slots_here, span, kv_here, HD)
        scores = jnp.einsum("skgd,stkd->skgt", query_heads, keys, preferred_element_type=f32) * scale
        position = head_place * span + jnp.arange(span, dtype=jnp.int32)
        live = position[None, :] < length_slot[:, None]
        weights = jnp.where(live[:, None, None, :], jnp.exp(scores), 0.0)
        own = jnp.exp(jnp.sum(query_heads.astype(f32) * key_own, axis=3) * scale)
        own = jnp.where(head_place == 0, own, 0.0)
        total = jnp.sum(weights, axis=3) + own
        mixed = jnp.einsum("skgt,stkd->skgd", weights.astype(bf16), values, preferred_element_type=f32)
        mixed = (mixed + own[..., None] * value_own).reshape(slots_here, q_here, HD)
        total = total.reshape(slots_here, q_here)

        gains = gain.astype(bf16).reshape(1, -1)
        step = n_head // 2
        while step:
            upper = (head_place & step) != 0
            half = total.shape[1] // 2
            keep_mix = jnp.where(upper, mixed[:, half:], mixed[:, :half])
            send_mix = jnp.where(upper, mixed[:, :half], mixed[:, half:])
            keep_tot = jnp.where(upper, total[:, half:], total[:, :half])
            send_tot = jnp.where(upper, total[:, :half], total[:, half:])
            tot_hi = send_tot.astype(bf16)
            tot_lo = (send_tot - tot_hi.astype(f32)).astype(bf16)
            flat = half * HD
            sent = jnp.concatenate(
                [
                    send_mix.astype(bf16).reshape(slots_here, flat),
                    tot_hi,
                    tot_lo,
                    gains.reshape(slots_here, -1),
                ],
                1,
            )
            came = rounds.swap(sent, "head", n_head, step)
            mixed = keep_mix + came[:, :flat].reshape(slots_here, half, HD).astype(f32)
            total = keep_tot + came[:, flat : flat + half].astype(f32)
            total = total + came[:, flat + half : flat + 2 * half].astype(f32)
            other = came[:, flat + 2 * half :].reshape(gains.shape)
            gains = jnp.concatenate(
                [jnp.where(upper, other, gains), jnp.where(upper, gains, other)], 0
            )
            step //= 2
        attended = (mixed / total[:, :, None]).astype(bf16).reshape(slots_here, -1)
        mine = jnp.concatenate([attended, gains.reshape(slots_here, -1)], 1)
        every = gather(rounds, mine, "pool", n_pool, 0)
        outputs, gains = every[:, : attended.shape[1]], every[:, attended.shape[1] :]
        order = slot_of[:, None] == jnp.arange(requests, dtype=jnp.int32)[None, :]

        chunk = hidden.shape[1]
        place = (head_place * n_aux + aux_place).reshape(1)
        term, message = project(
            outputs, order.astype(f32), out_proj[0], hidden, place, gains
        )
        width = term.shape[1]
        step = 1
        while step < n_aux:
            upper = (aux_place & step) != 0
            came = rounds.swap(message, "aux", n_aux, step)
            term = term + came[:, :width].astype(f32)
            other = came[:, width:]
            gains = jnp.stack([jnp.where(upper, other, gains), jnp.where(upper, gains, other)])
            step *= 2
            if step < n_aux:
                gains = gains.reshape(requests, -1)
                message = jnp.concatenate([term.astype(bf16), gains], 1)
        step = 1
        while step < n_head:
            term = term + rounds.swap(term.astype(bf16), "head", n_head, step).astype(f32)
            step *= 2
        stream = term.astype(bf16)

        bits = n_head.bit_length() - 1
        stored = gains.reshape((n_aux, n_pool) + (2,) * bits + (chunk,))
        turn = (1,) + tuple(range(1 + bits, 1, -1)) + (0, 2 + bits)
        full_gain = jnp.transpose(stored, turn).reshape(-1).astype(f32)

        full = gather(rounds, stream, "pool", n_pool, 1).astype(f32)
        mean_sq = jnp.mean(full * full, axis=1, keepdims=True)
        normed = (full * lax.rsqrt(mean_sq + 1e-05) * full_gain[None, :]).astype(bf16)
        logits, sums = score(normed, rounds.resident, lm_head)
        sums = total_over(rounds, sums, (("aux", n_aux), ("head", n_head), ("pool", n_pool)))
        entropy = jnp.log(sums[:, 0]) - sums[:, 1] / sums[:, 0]
        return (logits, entropy)

    return per_device


def solution(mesh):
    in_specs = (
        P("grp", ("pool", "head", "aux")),
        P(("pool", "head", "aux")),
        P(("grp", "pool"), "aux"),
        P(("grp", "pool"), "aux"),
        P(("grp", "pool"), "aux"),
        P(("grp", "pool"), "head", "aux"),
        P(("grp", "pool"), "head", "aux"),
        P("grp"),
        P("grp"),
        P("aux", "head", "pool"),
        P(None, ("pool", "head", "aux")),
    )
    out_specs = (P("grp", ("pool", "head", "aux")), P("grp"))
    return jax.shard_map(
        make_per_device(dict(mesh.shape)),
        mesh=mesh,
        in_specs=in_specs,
        out_specs=out_specs,
        check_vma=False,
    )
```

profile of v0, /device:TPU:0, one launch (start us, length us, event | category | flops | bytes accessed | tf_op | source)
XLA Modules:
  0.0 125.6 jit_solution(14371779575536206803)
XLA Ops:
  2.8 3.1 %collective-permute-start = (bf16[2,5120]{1,0:T(2,128)(2,1)S(1)}, bf16[2,5120]{1,0:T(2,128)(2,1)S(1)}, u32[]{:S(2)}, u32[]{:S(2)}) collective-permute-start(bf16[2,5120]{1,0:T(2,128)(2,1)S(1)} %join.1), channel_id=1, source_target_pairs={{0,4},{4,0},{8,12},{12,8},{1,5},{5,1},{9,13},{13,9},{2,6},{6,2},{1... | collective-permute-start | bytes 61448 | tf_op jit(solution)/shard_map/ppermute | solution.py:23
  7.7 3.1 %collective-permute-start.1 = (bf16[4,5120]{1,0:T(4,128)(2,1)S(1)}, bf16[4,5120]{1,0:T(4,128)(2,1)S(1)}, u32[]{:S(2)}, u32[]{:S(2)}) collective-permute-start(bf16[4,5120]{1,0:T(4,128)(2,1)S(1)} %pad_maximum_fusion.2), channel_id=1, source_target_pairs={{0,8},{4,12},{8,0},{12,4},{1,9},{5,13},{9,1},{13,5},{2,10},{6,14},... | collective-permute-start | bytes 122888 | tf_op jit(solution)/shard_map/ppermute | solution.py:23
  11.6 1.2 collective-permute-done.1
  14.4 1.2 fusion.2
  15.8 1.8 %collective-permute-start.2 = (bf16[2,2336]{1,0:T(2,128)(2,1)S(1)}, bf16[2,2336]{1,0:T(2,128)(2,1)S(1)}, u32[]{:S(2)}, u32[]{:S(2)}) collective-permute-start(bf16[2,2336]{1,0:T(2,128)(2,1)S(1)} %concatenate.30), channel_id=1, source_target_pairs={{0,2},{2,0},{1,3},{3,1},{4,6},{6,4},{5,7},{7,5},{8,10},{10,8},{9,1... | collective-permute-start | bytes 28040 | tf_op jit(solution)/shard_map/ppermute | solution.py:23
  17.6 1.8 %collective-permute-done.2 = bf16[2,2336]{1,0:T(2,128)(2,1)S(1)} collective-permute-done((bf16[2,2336]{1,0:T(2,128)(2,1)S(1)}, bf16[2,2336]{1,0:T(2,128)(2,1)S(1)}, u32[]{:S(2)}, u32[]{:S(2)}) %collective-permute-start.2) | collective-permute-done | bytes 9376 | tf_op jit(solution)/shard_map/ppermute | solution.py:23
  20.4 2.0 %collective-permute-start.3 = (bf16[2,2560]{1,0:T(2,128)(2,1)S(1)}, bf16[2,2560]{1,0:T(2,128)(2,1)S(1)}, u32[]{:S(2)}, u32[]{:S(2)}) collective-permute-start(bf16[2,2560]{1,0:T(2,128)(2,1)S(1)} %maximum_maximum_fusion), channel_id=1, source_target_pairs={{0,4},{4,0},{8,12},{12,8},{1,5},{5,1},{9,13},{13,9},{2,6},{6,2},{1... | collective-permute-start | bytes 30728 | tf_op jit(solution)/shard_map/ppermute | solution.py:23
  22.4 1.8 %collective-permute-done.3 = bf16[2,2560]{1,0:T(2,128)(2,1)S(1)} collective-permute-done((bf16[2,2560]{1,0:T(2,128)(2,1)S(1)}, bf16[2,2560]{1,0:T(2,128)(2,1)S(1)}, u32[]{:S(2)}, u32[]{:S(2)}) %collective-permute-start.3) | collective-permute-done | bytes 10272 | tf_op jit(solution)/shard_map/ppermute | solution.py:23
  24.2 3.0 %collective-permute-start.4 = (bf16[4,2560]{1,0:T(4,128)(2,1)S(1)}, bf16[4,2560]{1,0:T(4,128)(2,1)S(1)}, u32[]{:S(2)}, u32[]{:S(2)}) collective-permute-start(bf16[4,2560]{1,0:T(4,128)(2,1)S(1)} %pad_maximum_fusion.3), channel_id=1, source_target_pairs={{0,8},{4,12},{8,0},{12,4},{1,9},{5,13},{9,1},{13,5},{2,10},{6,14},... | collective-permute-start | bytes 61448 | tf_op jit(solution)/shard_map/ppermute | solution.py:23
  29.1 3.4 %copy-done.17 = bf16[1,2048,2048]{2,1,0:T(8,128)(2,1)S(1)} copy-done((bf16[1,2048,2048]{2,1,0:T(8,128)(2,1)S(1)}, bf16[1,2048,2048]{2,1,0:T(8,128)(2,1)}, u32[]{:S(2)}) %copy-start.17) | copy-done | bytes 8388632
  33.2 1.2 project.1
  34.5 1.2 collective-permute-done.5
  36.3 1.8 %collective-permute-start.6 = (bf16[8,2048]{1,0:T(8,128)(2,1)}, bf16[8,2048]{1,0:T(8,128)(2,1)}, u32[]{:S(2)}, u32[]{:S(2)}) collective-permute-start(bf16[8,2048]{1,0:T(8,128)(2,1)} %fusion.13), channel_id=1, source_target_pairs={{0,2},{2,0},{1,3},{3,1},{4,6},{6,4},{5,7},{7,5},{8,10},{10,8},{9,1... | collective-permute-start | bytes 98312 | tf_op jit(solution)/shard_map/ppermute | solution.py:23
  38.1 2.2 %shard_map.128.refs_6_ = bf16[512,4096]{1,0:T(8,128)(2,1)S(1)} custom-call(bf16[8192,4096]{1,0:T(8,128)(2,1)} %refs_8_.1), custom_call_target="tpu_custom_call" | custom-call | bytes 4194304 | tf_op jit(solution)/shard_map/pallas_call | solution.py:65
  40.4 2.0 %copy-done.1 = bf16[512,4096]{1,0:T(8,128)(2,1)} copy-done((bf16[512,4096]{1,0:T(8,128)(2,1)}, bf16[512,4096]{1,0:T(8,128)(2,1)S(1)}, u32[]{:S(2)}) %copy-start.1) | copy-done | bytes 4194328
  42.4 2.2 %shard_map.127.refs_5_ = bf16[512,4096]{1,0:T(8,128)(2,1)S(1)} custom-call(bf16[8192,4096]{1,0:T(8,128)(2,1)} %refs_8_.1), custom_call_target="tpu_custom_call" | custom-call | bytes 4194304 | tf_op jit(solution)/shard_map/pallas_call | solution.py:65
  44.6 2.0 %copy-done.3 = bf16[512,4096]{1,0:T(8,128)(2,1)} copy-done((bf16[512,4096]{1,0:T(8,128)(2,1)}, bf16[512,4096]{1,0:T(8,128)(2,1)S(1)}, u32[]{:S(2)}) %copy-start.3) | copy-done | bytes 4194328
  46.6 2.2 %shard_map.126.refs_4_ = bf16[512,4096]{1,0:T(8,128)(2,1)S(1)} custom-call(bf16[8192,4096]{1,0:T(8,128)(2,1)} %refs_8_.1), custom_call_target="tpu_custom_call" | custom-call | bytes 4194304 | tf_op jit(solution)/shard_map/pallas_call | solution.py:65
  48.8 2.0 %copy-done.5 = bf16[512,4096]{1,0:T(8,128)(2,1)} copy-done((bf16[512,4096]{1,0:T(8,128)(2,1)}, bf16[512,4096]{1,0:T(8,128)(2,1)S(1)}, u32[]{:S(2)}) %copy-start.5) | copy-done | bytes 4194328
  50.8 2.2 %shard_map.125.refs_3_ = bf16[512,4096]{1,0:T(8,128)(2,1)S(1)} custom-call(bf16[8192,4096]{1,0:T(8,128)(2,1)} %refs_8_.1), custom_call_target="tpu_custom_call" | custom-call | bytes 4194304 | tf_op jit(solution)/shard_map/pallas_call | solution.py:65
  53.0 1.9 %copy-done.7 = bf16[512,4096]{1,0:T(8,128)(2,1)} copy-done((bf16[512,4096]{1,0:T(8,128)(2,1)}, bf16[512,4096]{1,0:T(8,128)(2,1)S(1)}, u32[]{:S(2)}) %copy-start.7) | copy-done | bytes 4194328
  55.0 2.2 %shard_map.124.refs_2_ = bf16[512,4096]{1,0:T(8,128)(2,1)S(1)} custom-call(bf16[8192,4096]{1,0:T(8,128)(2,1)} %refs_8_.1), custom_call_target="tpu_custom_call" | custom-call | bytes 4194304 | tf_op jit(solution)/shard_map/pallas_call | solution.py:65
  57.2 2.0 %copy-done.9 = bf16[512,4096]{1,0:T(8,128)(2,1)} copy-done((bf16[512,4096]{1,0:T(8,128)(2,1)}, bf16[512,4096]{1,0:T(8,128)(2,1)S(1)}, u32[]{:S(2)}) %copy-start.9) | copy-done | bytes 4194328
  59.2 2.2 %shard_map.123.refs_1_ = bf16[512,4096]{1,0:T(8,128)(2,1)S(1)} custom-call(bf16[8192,4096]{1,0:T(8,128)(2,1)} %refs_8_.1), custom_call_target="tpu_custom_call" | custom-call | bytes 4194304 | tf_op jit(solution)/shard_map/pallas_call | solution.py:65
  61.4 2.0 %copy-done.11 = bf16[512,4096]{1,0:T(8,128)(2,1)} copy-done((bf16[512,4096]{1,0:T(8,128)(2,1)}, bf16[512,4096]{1,0:T(8,128)(2,1)S(1)}, u32[]{:S(2)}) %copy-start.11) | copy-done | bytes 4194328
  63.4 2.2 %shard_map.122.refs_0_ = bf16[512,4096]{1,0:T(8,128)(2,1)S(1)} custom-call(bf16[8192,4096]{1,0:T(8,128)(2,1)} %refs_8_.1), custom_call_target="tpu_custom_call" | custom-call | bytes 4194304 | tf_op jit(solution)/shard_map/pallas_call | solution.py:65
  65.7 2.0 %copy-done.13 = bf16[512,4096]{1,0:T(8,128)(2,1)} copy-done((bf16[512,4096]{1,0:T(8,128)(2,1)}, bf16[512,4096]{1,0:T(8,128)(2,1)S(1)}, u32[]{:S(2)}) %copy-start.13) | copy-done | bytes 4194328
  67.6 2.2 %shard_map.129.refs_7_ = bf16[512,4096]{1,0:T(8,128)(2,1)S(1)} custom-call(bf16[8192,4096]{1,0:T(8,128)(2,1)} %refs_8_.1), custom_call_target="tpu_custom_call" | custom-call | bytes 4194304 | tf_op jit(solution)/shard_map/pallas_call | solution.py:65
  69.9 2.0 %copy-done.15 = bf16[512,4096]{1,0:T(8,128)(2,1)} copy-done((bf16[512,4096]{1,0:T(8,128)(2,1)}, bf16[512,4096]{1,0:T(8,128)(2,1)S(1)}, u32[]{:S(2)}) %copy-start.15) | copy-done | bytes 4194328
  72.6 1.6 %collective-permute-start.7 = (bf16[8,2048]{1,0:T(8,128)(2,1)S(1)}, bf16[8,2048]{1,0:T(8,128)(2,1)S(1)}, u32[]{:S(2)}, u32[]{:S(2)}) collective-permute-start(bf16[8,2048]{1,0:T(8,128)(2,1)S(1)} %add_convert_fusion), channel_id=1, source_target_pairs={{0,4},{4,0},{8,12},{12,8},{1,5},{5,1},{9,13},{13,9},{2,6},{6,2},{1... | collective-permute-start | bytes 98312 | tf_op jit(solution)/shard_map/ppermute | solution.py:23
  74.3 2.3 %collective-permute-done.7 = bf16[8,2048]{1,0:T(8,128)(2,1)S(1)} collective-permute-done((bf16[8,2048]{1,0:T(8,128)(2,1)S(1)}, bf16[8,2048]{1,0:T(8,128)(2,1)S(1)}, u32[]{:S(2)}, u32[]{:S(2)}) %collective-permute-start.7) | collective-permute-done | bytes 32800 | tf_op jit(solution)/shard_map/ppermute | solution.py:23
  76.6 2.7 %collective-permute-start.8 = (bf16[8,4096]{1,0:T(8,128)(2,1)S(1)}, bf16[8,4096]{1,0:T(8,128)(2,1)S(1)}, u32[]{:S(2)}, u32[]{:S(2)}) collective-permute-start(bf16[8,4096]{1,0:T(8,128)(2,1)S(1)} %pad_maximum_fusion.1), channel_id=1, source_target_pairs={{0,8},{4,12},{8,0},{12,4},{1,9},{5,13},{9,1},{13,5},{2,10},{6,14},... | collective-permute-start | bytes 196616 | tf_op jit(solution)/shard_map/ppermute | solution.py:23
  79.4 2.5 %collective-permute-done.8 = bf16[8,4096]{1,0:T(8,128)(2,1)S(1)} collective-permute-done((bf16[8,4096]{1,0:T(8,128)(2,1)S(1)}, bf16[8,4096]{1,0:T(8,128)(2,1)S(1)}, u32[]{:S(2)}, u32[]{:S(2)}) %collective-permute-start.8) | collective-permute-done | bytes 65568 | tf_op jit(solution)/shard_map/ppermute | solution.py:23
  82.2 2.2 %copy-done.2 = bf16[512,4096]{1,0:T(8,128)(2,1)S(1)} copy-done((bf16[512,4096]{1,0:T(8,128)(2,1)S(1)}, bf16[512,4096]{1,0:T(8,128)(2,1)}, u32[]{:S(2)}) %copy-start.2) | copy-done | bytes 4194328
  84.4 2.2 %copy-done.4 = bf16[512,4096]{1,0:T(8,128)(2,1)S(1)} copy-done((bf16[512,4096]{1,0:T(8,128)(2,1)S(1)}, bf16[512,4096]{1,0:T(8,128)(2,1)}, u32[]{:S(2)}) %copy-start.4) | copy-done | bytes 4194328
  86.6 2.2 %copy-done.6 = bf16[512,4096]{1,0:T(8,128)(2,1)S(1)} copy-done((bf16[512,4096]{1,0:T(8,128)(2,1)S(1)}, bf16[512,4096]{1,0:T(8,128)(2,1)}, u32[]{:S(2)}) %copy-start.6) | copy-done | bytes 4194328
  88.8 2.2 %copy-done.8 = bf16[512,4096]{1,0:T(8,128)(2,1)S(1)} copy-done((bf16[512,4096]{1,0:T(8,128)(2,1)S(1)}, bf16[512,4096]{1,0:T(8,128)(2,1)}, u32[]{:S(2)}) %copy-start.8) | copy-done | bytes 4194328
  91.0 2.2 %copy-done.10 = bf16[512,4096]{1,0:T(8,128)(2,1)S(1)} copy-done((bf16[512,4096]{1,0:T(8,128)(2,1)S(1)}, bf16[512,4096]{1,0:T(8,128)(2,1)}, u32[]{:S(2)}) %copy-start.10) | copy-done | bytes 4194328
  93.2 2.2 %copy-done.12 = bf16[512,4096]{1,0:T(8,128)(2,1)S(1)} copy-done((bf16[512,4096]{1,0:T(8,128)(2,1)S(1)}, bf16[512,4096]{1,0:T(8,128)(2,1)}, u32[]{:S(2)}) %copy-start.12) | copy-done | bytes 4194328
  95.3 2.2 %copy-done.14 = bf16[512,4096]{1,0:T(8,128)(2,1)S(1)} copy-done((bf16[512,4096]{1,0:T(8,128)(2,1)S(1)}, bf16[512,4096]{1,0:T(8,128)(2,1)}, u32[]{:S(2)}) %copy-start.14) | copy-done | bytes 4194328
  97.5 2.2 %copy-done.16 = bf16[512,4096]{1,0:T(8,128)(2,1)S(1)} copy-done((bf16[512,4096]{1,0:T(8,128)(2,1)S(1)}, bf16[512,4096]{1,0:T(8,128)(2,1)}, u32[]{:S(2)}) %copy-start.16) | copy-done | bytes 4194328
  99.7 12.2 %score.1 = (f32[8,4096]{1,0:T(8,128)}, f32[8,128]{1,0:T(8,128)S(1)}) custom-call(bf16[8,8192]{1,0:T(8,128)(2,1)S(1)} %fusion.9.x_ref, bf16[512,4096]{1,0:T(8,128)(2,1)S(1)} %copy-done.14, bf16[512,4096]{1,0:T(8,128)(2,1)S(1)} %copy-done.12, bf16[512,4096]{1,0:T(8,128)(2,1)S(1)} %copy-done.10, bf16[512,4096]{1,0:T(8,128)(2,1)S(1)} %copy-done.8, ...), custom_call_target="tpu_custom_call" | custom-call | flops 536870912 | bytes 33554432 | tf_op jit(solution)/shard_map/score/pallas_call | solution.py:176
  112.0 1.2 collective-permute-done.9
  113.5 3.3 %collective-permute-done.10 = f32[8,128]{1,0:T(8,128)S(1)} collective-permute-done((f32[8,128]{1,0:T(8,128)S(1)}, f32[8,128]{1,0:T(8,128)S(1)}, u32[]{:S(2)}, u32[]{:S(2)}) %collective-permute-start.10) | collective-permute-done | bytes 4128 | tf_op jit(solution)/shard_map/ppermute | solution.py:21
  116.8 1.6 %collective-permute-start.11 = (f32[8,128]{1,0:T(8,128)S(1)}, f32[8,128]{1,0:T(8,128)S(1)}, u32[]{:S(2)}, u32[]{:S(2)}) collective-permute-start(f32[8,128]{1,0:T(8,128)S(1)} %add.83), channel_id=1, source_target_pairs={{0,4},{4,0},{8,12},{12,8},{1,5},{5,1},{9,13},{13,9},{2,6},{6,2},{1... | collective-permute-start | bytes 12296 | tf_op jit(solution)/shard_map/ppermute | solution.py:21
  118.4 2.0 %collective-permute-done.11 = f32[8,128]{1,0:T(8,128)S(1)} collective-permute-done((f32[8,128]{1,0:T(8,128)S(1)}, f32[8,128]{1,0:T(8,128)S(1)}, u32[]{:S(2)}, u32[]{:S(2)}) %collective-permute-start.11) | collective-permute-done | bytes 4128 | tf_op jit(solution)/shard_map/ppermute | solution.py:21
  120.4 2.8 %collective-permute-start.12 = (f32[8,128]{1,0:T(8,128)S(1)}, f32[8,128]{1,0:T(8,128)S(1)}, u32[]{:S(2)}, u32[]{:S(2)}) collective-permute-start(f32[8,128]{1,0:T(8,128)S(1)} %add.84), channel_id=1, source_target_pairs={{0,8},{4,12},{8,0},{12,4},{1,9},{5,13},{9,1},{13,5},{2,10},{6,14},... | collective-permute-start | bytes 12296 | tf_op jit(solution)/shard_map/ppermute | solution.py:21
  123.2 1.7 %collective-permute-done.12 = f32[8,128]{1,0:T(8,128)S(1)} collective-permute-done((f32[8,128]{1,0:T(8,128)S(1)}, f32[8,128]{1,0:T(8,128)S(1)}, u32[]{:S(2)}, u32[]{:S(2)}) %collective-permute-start.12) | collective-permute-done | bytes 4128 | tf_op jit(solution)/shard_map/ppermute | solution.py:21
  (102 shorter events, 13.0 us)
Async XLA Ops:
  0.6 13.3 %copy-start = (bf16[2,256,512]{2,1,0:T(8,128)(2,1)S(1)}, bf16[2,256,512]{2,1,0:T(8,128)(2,1)}, u32[]{:S(2)}) copy-start(bf16[2,256,512]{2,1,0:T(8,128)(2,1)} %param.16) | copy-start | bytes 1572868
  0.6 0.8 copy-start.22
  1.4 0.7 copy-start.24
  2.1 0.7 copy-start.25
  2.8 4.8 %collective-permute-start = (bf16[2,5120]{1,0:T(2,128)(2,1)S(1)}, bf16[2,5120]{1,0:T(2,128)(2,1)S(1)}, u32[]{:S(2)}, u32[]{:S(2)}) collective-permute-start(bf16[2,5120]{1,0:T(2,128)(2,1)S(1)} %join.1), channel_id=1, source_target_pairs={{0,4},{4,0},{8,12},{12,8},{1,5},{5,1},{9,13},{13,9},{2,6},{6,2},{1... | collective-permute-start | bytes 61448 | tf_op jit(solution)/shard_map/ppermute | solution.py:23
  7.7 5.1 %collective-permute-start.1 = (bf16[4,5120]{1,0:T(4,128)(2,1)S(1)}, bf16[4,5120]{1,0:T(4,128)(2,1)S(1)}, u32[]{:S(2)}, u32[]{:S(2)}) collective-permute-start(bf16[4,5120]{1,0:T(4,128)(2,1)S(1)} %pad_maximum_fusion.2), channel_id=1, source_target_pairs={{0,8},{4,12},{8,0},{12,4},{1,9},{5,13},{9,1},{13,5},{2,10},{6,14},... | collective-permute-start | bytes 122888 | tf_op jit(solution)/shard_map/ppermute | solution.py:23
  15.8 3.7 %collective-permute-start.2 = (bf16[2,2336]{1,0:T(2,128)(2,1)S(1)}, bf16[2,2336]{1,0:T(2,128)(2,1)S(1)}, u32[]{:S(2)}, u32[]{:S(2)}) collective-permute-start(bf16[2,2336]{1,0:T(2,128)(2,1)S(1)} %concatenate.30), channel_id=1, source_target_pairs={{0,2},{2,0},{1,3},{3,1},{4,6},{6,4},{5,7},{7,5},{8,10},{10,8},{9,1... | collective-permute-start | bytes 28040 | tf_op jit(solution)/shard_map/ppermute | solution.py:23
  20.4 3.7 %collective-permute-start.3 = (bf16[2,2560]{1,0:T(2,128)(2,1)S(1)}, bf16[2,2560]{1,0:T(2,128)(2,1)S(1)}, u32[]{:S(2)}, u32[]{:S(2)}) collective-permute-start(bf16[2,2560]{1,0:T(2,128)(2,1)S(1)} %maximum_maximum_fusion), channel_id=1, source_target_pairs={{0,4},{4,0},{8,12},{12,8},{1,5},{5,1},{9,13},{13,9},{2,6},{6,2},{1... | collective-permute-start | bytes 30728 | tf_op jit(solution)/shard_map/ppermute | solution.py:23
  24.2 4.8 %collective-permute-start.4 = (bf16[4,2560]{1,0:T(4,128)(2,1)S(1)}, bf16[4,2560]{1,0:T(4,128)(2,1)S(1)}, u32[]{:S(2)}, u32[]{:S(2)}) collective-permute-start(bf16[4,2560]{1,0:T(4,128)(2,1)S(1)} %pad_maximum_fusion.3), channel_id=1, source_target_pairs={{0,8},{4,12},{8,0},{12,4},{1,9},{5,13},{9,1},{13,5},{2,10},{6,14},... | collective-permute-start | bytes 61448 | tf_op jit(solution)/shard_map/ppermute | solution.py:23
  29.1 5.4 %copy-start.20 = (bf16[8,512]{1,0:T(8,128)(2,1)}, bf16[8,512]{1,0:T(8,128)(2,1)S(1)}, u32[]{:S(2)}) copy-start(bf16[8,512]{1,0:T(8,128)(2,1)S(1)} %pad_maximum_fusion.4.gain_ref) | copy-start | bytes 24580
  29.1 3.4 %copy-start.17 = (bf16[1,2048,2048]{2,1,0:T(8,128)(2,1)S(1)}, bf16[1,2048,2048]{2,1,0:T(8,128)(2,1)}, u32[]{:S(2)}) copy-start(bf16[1,2048,2048]{2,1,0:T(8,128)(2,1)} %param.20) | copy-start | bytes 25165828
  32.5 0.7 copy-start.23
  34.4 1.3 %copy-start.18 = (f32[8,2048]{1,0:T(8,128)}, f32[8,2048]{1,0:T(8,128)S(1)}, u32[]{:S(2)}) copy-start(f32[8,2048]{1,0:T(8,128)S(1)} %get-tuple-element.6) | copy-start | bytes 196612
  34.4 1.3 %collective-permute-start.5 = (bf16[8,2560]{1,0:T(8,128)(2,1)S(1)}, bf16[8,2560]{1,0:T(8,128)(2,1)S(1)}, u32[]{:S(2)}, u32[]{:S(2)}) collective-permute-start(bf16[8,2560]{1,0:T(8,128)(2,1)S(1)} %get-tuple-element.7), channel_id=1, source_target_pairs={{0,1},{1,0},{2,3},{3,2},{4,5},{5,4},{6,7},{7,6},{8,9},{9,8},{10,11... | collective-permute-start | bytes 122888 | tf_op jit(solution)/shard_map/ppermute | solution.py:21
  35.7 0.6 copy-start.26
  36.3 35.5 %collective-permute-start.6 = (bf16[8,2048]{1,0:T(8,128)(2,1)}, bf16[8,2048]{1,0:T(8,128)(2,1)}, u32[]{:S(2)}, u32[]{:S(2)}) collective-permute-start(bf16[8,2048]{1,0:T(8,128)(2,1)} %fusion.13), channel_id=1, source_target_pairs={{0,2},{2,0},{1,3},{3,1},{4,6},{6,4},{5,7},{7,5},{8,10},{10,8},{9,1... | collective-permute-start | bytes 98312 | tf_op jit(solution)/shard_map/ppermute | solution.py:23
  40.3 2.0 %copy-start.1 = (bf16[512,4096]{1,0:T(8,128)(2,1)}, bf16[512,4096]{1,0:T(8,128)(2,1)S(1)}, u32[]{:S(2)}) copy-start(bf16[512,4096]{1,0:T(8,128)(2,1)S(1)} %shard_map.128.refs_6_) | copy-start | bytes 12582916
  44.6 2.0 %copy-start.3 = (bf16[512,4096]{1,0:T(8,128)(2,1)}, bf16[512,4096]{1,0:T(8,128)(2,1)S(1)}, u32[]{:S(2)}) copy-start(bf16[512,4096]{1,0:T(8,128)(2,1)S(1)} %shard_map.127.refs_5_) | copy-start | bytes 12582916
  48.8 2.0 %copy-start.5 = (bf16[512,4096]{1,0:T(8,128)(2,1)}, bf16[512,4096]{1,0:T(8,128)(2,1)S(1)}, u32[]{:S(2)}) copy-start(bf16[512,4096]{1,0:T(8,128)(2,1)S(1)} %shard_map.126.refs_4_) | copy-start | bytes 12582916
  53.0 1.9 %copy-start.7 = (bf16[512,4096]{1,0:T(8,128)(2,1)}, bf16[512,4096]{1,0:T(8,128)(2,1)S(1)}, u32[]{:S(2)}) copy-start(bf16[512,4096]{1,0:T(8,128)(2,1)S(1)} %shard_map.125.refs_3_) | copy-start | bytes 12582916
  57.2 2.0 %copy-start.9 = (bf16[512,4096]{1,0:T(8,128)(2,1)}, bf16[512,4096]{1,0:T(8,128)(2,1)S(1)}, u32[]{:S(2)}) copy-start(bf16[512,4096]{1,0:T(8,128)(2,1)S(1)} %shard_map.124.refs_2_) | copy-start | bytes 12582916
  61.4 2.0 %copy-start.11 = (bf16[512,4096]{1,0:T(8,128)(2,1)}, bf16[512,4096]{1,0:T(8,128)(2,1)S(1)}, u32[]{:S(2)}) copy-start(bf16[512,4096]{1,0:T(8,128)(2,1)S(1)} %shard_map.123.refs_1_) | copy-start | bytes 12582916
  65.6 2.0 %copy-start.13 = (bf16[512,4096]{1,0:T(8,128)(2,1)}, bf16[512,4096]{1,0:T(8,128)(2,1)S(1)}, u32[]{:S(2)}) copy-start(bf16[512,4096]{1,0:T(8,128)(2,1)S(1)} %shard_map.122.refs_0_) | copy-start | bytes 12582916
  67.6 4.2 %copy-start.19 = (f32[8,2048]{1,0:T(8,128)S(1)}, f32[8,2048]{1,0:T(8,128)}, u32[]{:S(2)}) copy-start(f32[8,2048]{1,0:T(8,128)} %copy-done.18) | copy-start | bytes 196612
  67.6 4.2 %copy-start.27 = (bf16[8,2560]{1,0:T(8,128)(2,1)S(1)}, bf16[8,2560]{1,0:T(8,128)(2,1)}, u32[]{:S(2)}) copy-start(bf16[8,2560]{1,0:T(8,128)(2,1)} %copy-done.26) | copy-start | bytes 122884
  67.6 6.7 %copy-start.21 = (bf16[8,512]{1,0:T(8,128)(2,1)S(1)}, bf16[8,512]{1,0:T(8,128)(2,1)}, u32[]{:S(2)}) copy-start(bf16[8,512]{1,0:T(8,128)(2,1)} %copy-done.20) | copy-start | bytes 24580
  69.9 2.0 %copy-start.15 = (bf16[512,4096]{1,0:T(8,128)(2,1)}, bf16[512,4096]{1,0:T(8,128)(2,1)S(1)}, u32[]{:S(2)}) copy-start(bf16[512,4096]{1,0:T(8,128)(2,1)S(1)} %shard_map.129.refs_7_) | copy-start | bytes 12582916
  72.6 4.0 %collective-permute-start.7 = (bf16[8,2048]{1,0:T(8,128)(2,1)S(1)}, bf16[8,2048]{1,0:T(8,128)(2,1)S(1)}, u32[]{:S(2)}, u32[]{:S(2)}) collective-permute-start(bf16[8,2048]{1,0:T(8,128)(2,1)S(1)} %add_convert_fusion), channel_id=1, source_target_pairs={{0,4},{4,0},{8,12},{12,8},{1,5},{5,1},{9,13},{13,9},{2,6},{6,2},{1... | collective-permute-start | bytes 98312 | tf_op jit(solution)/shard_map/ppermute | solution.py:23
  76.6 5.2 %collective-permute-start.8 = (bf16[8,4096]{1,0:T(8,128)(2,1)S(1)}, bf16[8,4096]{1,0:T(8,128)(2,1)S(1)}, u32[]{:S(2)}, u32[]{:S(2)}) collective-permute-start(bf16[8,4096]{1,0:T(8,128)(2,1)S(1)} %pad_maximum_fusion.1), channel_id=1, source_target_pairs={{0,8},{4,12},{8,0},{12,4},{1,9},{5,13},{9,1},{13,5},{2,10},{6,14},... | collective-permute-start | bytes 196616 | tf_op jit(solution)/shard_map/ppermute | solution.py:23
  82.2 2.2 %copy-start.2 = (bf16[512,4096]{1,0:T(8,128)(2,1)S(1)}, bf16[512,4096]{1,0:T(8,128)(2,1)}, u32[]{:S(2)}) copy-start(bf16[512,4096]{1,0:T(8,128)(2,1)} %copy-done.1) | copy-start | bytes 12582916
  84.4 2.2 %copy-start.4 = (bf16[512,4096]{1,0:T(8,128)(2,1)S(1)}, bf16[512,4096]{1,0:T(8,128)(2,1)}, u32[]{:S(2)}) copy-start(bf16[512,4096]{1,0:T(8,128)(2,1)} %copy-done.3) | copy-start | bytes 12582916
  86.6 2.2 %copy-start.6 = (bf16[512,4096]{1,0:T(8,128)(2,1)S(1)}, bf16[512,4096]{1,0:T(8,128)(2,1)}, u32[]{:S(2)}) copy-start(bf16[512,4096]{1,0:T(8,128)(2,1)} %copy-done.5) | copy-start | bytes 12582916
  88.8 2.2 %copy-start.8 = (bf16[512,4096]{1,0:T(8,128)(2,1)S(1)}, bf16[512,4096]{1,0:T(8,128)(2,1)}, u32[]{:S(2)}) copy-start(bf16[512,4096]{1,0:T(8,128)(2,1)} %copy-done.7) | copy-start | bytes 12582916
  91.0 2.2 %copy-start.10 = (bf16[512,4096]{1,0:T(8,128)(2,1)S(1)}, bf16[512,4096]{1,0:T(8,128)(2,1)}, u32[]{:S(2)}) copy-start(bf16[512,4096]{1,0:T(8,128)(2,1)} %copy-done.9) | copy-start | bytes 12582916
  93.1 2.2 %copy-start.12 = (bf16[512,4096]{1,0:T(8,128)(2,1)S(1)}, bf16[512,4096]{1,0:T(8,128)(2,1)}, u32[]{:S(2)}) copy-start(bf16[512,4096]{1,0:T(8,128)(2,1)} %copy-done.11) | copy-start | bytes 12582916
  95.3 2.2 %copy-start.14 = (bf16[512,4096]{1,0:T(8,128)(2,1)S(1)}, bf16[512,4096]{1,0:T(8,128)(2,1)}, u32[]{:S(2)}) copy-start(bf16[512,4096]{1,0:T(8,128)(2,1)} %copy-done.13) | copy-start | bytes 12582916
  97.5 2.2 %copy-start.16 = (bf16[512,4096]{1,0:T(8,128)(2,1)S(1)}, bf16[512,4096]{1,0:T(8,128)(2,1)}, u32[]{:S(2)}) copy-start(bf16[512,4096]{1,0:T(8,128)(2,1)} %copy-done.15) | copy-start | bytes 12582916
  112.0 1.2 collective-permute-start.9
  113.2 3.6 %collective-permute-start.10 = (f32[8,128]{1,0:T(8,128)S(1)}, f32[8,128]{1,0:T(8,128)S(1)}, u32[]{:S(2)}, u32[]{:S(2)}) collective-permute-start(f32[8,128]{1,0:T(8,128)S(1)} %add.82), channel_id=1, source_target_pairs={{0,2},{2,0},{1,3},{3,1},{4,6},{6,4},{5,7},{7,5},{8,10},{10,8},{9,1... | collective-permute-start | bytes 12296 | tf_op jit(solution)/shard_map/ppermute | solution.py:21
  116.8 3.6 %collective-permute-start.11 = (f32[8,128]{1,0:T(8,128)S(1)}, f32[8,128]{1,0:T(8,128)S(1)}, u32[]{:S(2)}, u32[]{:S(2)}) collective-permute-start(f32[8,128]{1,0:T(8,128)S(1)} %add.83), channel_id=1, source_target_pairs={{0,4},{4,0},{8,12},{12,8},{1,5},{5,1},{9,13},{13,9},{2,6},{6,2},{1... | collective-permute-start | bytes 12296 | tf_op jit(solution)/shard_map/ppermute | solution.py:21
  120.4 4.5 %collective-permute-start.12 = (f32[8,128]{1,0:T(8,128)S(1)}, f32[8,128]{1,0:T(8,128)S(1)}, u32[]{:S(2)}, u32[]{:S(2)}) collective-permute-start(f32[8,128]{1,0:T(8,128)S(1)} %add.84), channel_id=1, source_target_pairs={{0,8},{4,12},{8,0},{12,4},{1,9},{5,13},{9,1},{13,5},{2,10},{6,14},... | collective-permute-start | bytes 12296 | tf_op jit(solution)/shard_map/ppermute | solution.py:21
where the time goes:
time: 126 us
  local copies, waits for them, and re-layouts  40 us (32%)
  Pallas kernels  31.2 us (25%)
  starting transfers between devices  23.8 us (19%)
  waiting for transfers between devices  21 us (17%)
  other arithmetic  6.18 us (5%)
  matrix products  2.42 us (2%)
    unnamed x62, local copies, waits for them, and re-layouts  39.8 us
    ppermute x8, starting transfers between devices, swap(): y = lax.ppermute(x, axis, pairs)  19.1 us
    pallas_call x8, Pallas kernels, fetch(): pl.pallas_call(body, out_shape=pltpu.VMEM((rows, lm_head.shape[1]), lm_he...  17.7 us
    pallas_call x1, Pallas kernels, score(): pl.pallas_call(body, out_shape=(jax.ShapeDtypeStruct((requests, width), f...  12.2 us
    ppermute x8, waiting for transfers between devices, swap(): y = lax.ppermute(x, axis, pairs)  11.5 us
    ppermute x5, waiting for transfers between devices, swap(): return lax.ppermute(x, axis, pairs)  9.45 us
    ppermute x5, starting transfers between devices, swap(): return lax.ppermute(x, axis, pairs)  4.75 us
  transfers between devices with their start and end apart: 13, of which 12 were waited for; matrix products, arithmetic and copies ran while one was open for 2% of the time, Pallas kernels for 14%

commit v1 on v0

v1 whole, which is shorter than its diff:
```python
import math

import jax
import jax.numpy as jnp
from jax import lax
from jax.experimental import pallas as pl
from jax.experimental.pallas import tpu as pltpu
from jax.sharding import PartitionSpec as P

HD = 128
VM = pl.BlockSpec(memory_space=pltpu.VMEM)
HB = pl.BlockSpec(memory_space=pl.ANY)
MIB = 1 << 20
WINDOWS = 8
PIECES = 16
F32, BF16 = jnp.float32, jnp.bfloat16


def call(body, outs, ins, scratch=(), grant=2 * MIB, cost=None):
    return pl.pallas_call(
        body,
        out_shape=outs,
        in_specs=ins,
        out_specs=jax.tree.map(lambda _: VM, outs),
        scratch_shapes=list(scratch),
        cost_estimate=cost,
        compiler_params=pltpu.CompilerParams(vmem_limit_bytes=grant),
    )


def shaped(shape, dtype):
    return jax.ShapeDtypeStruct(tuple(shape), dtype)


def fetch(lm_head, piece):
    rows = lm_head.shape[0] // PIECES
    cuts = 4
    part = rows // cuts

    def body(src, dst, sem):
        copies = [
            pltpu.make_async_copy(
                src.at[pl.ds(piece * rows + i * part, part)],
                dst.at[pl.ds(i * part, part)],
                sem.at[i],
            )
            for i in range(cuts)
        ]
        for copy in copies:
            copy.start()
        for copy in copies:
            copy.wait()

    size = rows * lm_head.shape[1] * 2
    return call(
        body,
        pltpu.VMEM((rows, lm_head.shape[1]), lm_head.dtype),
        [HB],
        [pltpu.SemaphoreType.DMA((cuts,))],
        MIB,
        pl.CostEstimate(flops=0, bytes_accessed=size, transcendentals=0),
    )(lm_head)


class Rounds:
    def __init__(self, lm_head):
        self.lm_head = lm_head
        self.resident = []

    def swap(self, x, axis, size, step):
        pairs = [(i, i ^ step) for i in range(size)]
        if axis == "aux" or len(self.resident) == WINDOWS:
            return lax.ppermute(x, axis, pairs)
        at = len(self.resident)
        y = lax.ppermute(x, axis, pairs)
        self.resident.append(fetch(self.lm_head, at))
        return y


def steps_of(size):
    return [1 << i for i in range(size.bit_length() - 1)]


def is_upper(axis, step):
    return (lax.axis_index(axis) & step) != 0


def merge(x, y, axis, step, dim):
    size = x.shape[dim]

    def body(x_ref, y_ref, o_ref):
        upper = is_upper(axis, step)
        a, b = x_ref[...], y_ref[...]
        low, high = jnp.where(upper, b, a), jnp.where(upper, a, b)
        if dim == 0:
            o_ref[:size, :] = low
            o_ref[size:, :] = high
        else:
            o_ref[:, :size] = low
            o_ref[:, size:] = high

    shape = list(x.shape)
    shape[dim] *= 2
    return call(body, shaped(shape, x.dtype), [VM, VM])(x, y)


def gather(rounds, x, axis, size, dim):
    for step in steps_of(size):
        x = merge(x, rounds.swap(x, axis, size, step), axis, step, dim)
    return x


def join(*arrays):
    widths = [a.shape[1] for a in arrays]

    def body(*refs):
        out, sem = refs[-2:]
        copies, at = [], 0
        for i, width in enumerate(widths):
            copies.append(pltpu.make_async_copy(refs[i], out.at[:, at : at + width], sem.at[i]))
            at += width
        for copy in copies:
            copy.start()
        for copy in copies:
            copy.wait()

    return call(
        body,
        shaped((arrays[0].shape[0], sum(widths)), arrays[0].dtype),
        [pl.BlockSpec(memory_space=pltpu.HBM)] * len(arrays),
        [pltpu.SemaphoreType.DMA((len(arrays),))],
        MIB,
    )(*arrays)


def to_column(row):
    n = row.shape[1]
    diag = lax.broadcasted_iota(jnp.int32, (n, n), 0) == lax.broadcasted_iota(jnp.int32, (n, n), 1)
    return jnp.sum(jnp.where(diag, jnp.broadcast_to(row, (n, n)), 0), axis=1, keepdims=True)


def split_heads(mixes, totals, step, keep_ref, msg_ref):
    upper = is_upper("head", step)
    for s, (mix, total) in enumerate(zip(mixes, totals)):
        half = mix.shape[0] // 2
        keep_ref[s, :, :HD] = jnp.where(upper, mix[half:], mix[:half])
        keep_ref[s, :, HD:] = jnp.where(upper, total[half:], total[:half])
        send = jnp.where(upper, total[:half], total[half:])
        rough = send.astype(BF16)
        msg_ref[s, :, :HD] = jnp.where(upper, mix[:half], mix[half:]).astype(BF16)
        msg_ref[s, :, HD : 2 * HD] = rough
        msg_ref[s, :, 2 * HD :] = (send - rough.astype(F32)).astype(BF16)


def attend(every, slot_row, length_row, cache_key, cache_value, widths, step):
    slots, span, nk = cache_key.shape
    nq = widths[0]
    kv, heads = nk // HD, nq // HD
    group = heads // kv
    scale = 1.0 / math.sqrt(HD)

    def body(every_ref, slot_ref, length_ref, key_ref, value_ref, keep_ref, msg_ref):
        head_place = lax.axis_index("head")
        slot_col = to_column(slot_ref[...])
        length_col = to_column(length_ref[...])
        rows = every_ref[...].astype(F32)
        mixes, totals = [], []
        for s in range(slots):
            chosen = slot_col == lax.axis_index("pool") * slots + s
            row = jnp.sum(jnp.where(chosen, rows, 0.0), axis=0, keepdims=True)
            length = jnp.sum(jnp.where(chosen, length_col, 0), axis=0, keepdims=True)
            stacked = []
            for k in range(kv):
                at = k * group * HD
                piece = jnp.concatenate(
                    [row[:, at + g * HD : at + (g + 1) * HD] for g in range(group)], 0
                )
                stacked.append(piece)
            queries = jnp.concatenate(stacked, 0)
            wide = []
            for k in range(kv):
                blank = jnp.zeros((group, HD), F32)
                wide.append(jnp.concatenate([stacked[k] if c == k else blank for c in range(kv)], 1))
            wide = jnp.concatenate(wide, 0).astype(BF16)
            scores = scale * lax.dot_general(
                wide, key_ref[s], (((1,), (1,)), ((), ())), preferred_element_type=F32
            )
            position = head_place * span + lax.broadcasted_iota(jnp.int32, (heads, span), 1)
            weights = jnp.where(position < length, jnp.exp(scores), 0.0)
            total = jnp.sum(weights, axis=1, keepdims=True)
            full = jnp.dot(weights.astype(BF16), value_ref[s], preferred_element_type=F32)
            mix = jnp.concatenate(
                [full[k * group : (k + 1) * group, k * HD : (k + 1) * HD] for k in range(kv)], 0
            )

            def spread(offset):
                return jnp.concatenate(
                    [
                        jnp.broadcast_to(row[:, offset + k * HD : offset + (k + 1) * HD], (group, HD))
                        for k in range(kv)
                    ],
                    0,
                )

            own = jnp.exp(jnp.sum(queries * spread(nq), axis=1, keepdims=True) * scale)
            own = jnp.where(head_place == 0, own, 0.0)
            mixes.append(mix + own * spread(nq + nk))
            totals.append(jnp.broadcast_to(total + own, (heads, HD)))
        split_heads(mixes, totals, step, keep_ref, msg_ref)

    return call(
        body,
        (
            shaped((slots, heads // 2, 2 * HD), F32),
            shaped((slots, heads // 2, 3 * HD), BF16),
        ),
        [VM] * 5,
        grant=4 * MIB,
    )(every, slot_row, length_row, cache_key, cache_value)


def add_part(keep_ref, came_ref, s):
    came = came_ref[s].astype(F32)
    mix = keep_ref[s, :, :HD] + came[:, :HD]
    total = keep_ref[s, :, HD:] + came[:, HD : 2 * HD] + came[:, 2 * HD :]
    return mix, total


def split_again(keep, came, step):
    slots, heads = keep.shape[:2]

    def body(keep_in, came_ref, keep_ref, msg_ref):
        mixes, totals = zip(*[add_part(keep_in, came_ref, s) for s in range(slots)])
        split_heads(mixes, totals, step, keep_ref, msg_ref)

    return call(
        body,
        (shaped((slots, heads // 2, 2 * HD), F32), shaped((slots, heads // 2, 3 * HD), BF16)),
        [VM, VM],
    )(keep, came)


def finish(keep, came, gain_row):
    slots, heads = keep.shape[:2]
    chunk = gain_row.shape[1]

    def body(keep_ref, came_ref, gain_ref, msg_ref):
        rows = []
        for s in range(slots):
            mix, total = add_part(keep_ref, came_ref, s)
            out = mix / total
            rows.append(jnp.concatenate([out[j : j + 1, :] for j in range(heads)], 1))
        msg_ref[:, : heads * HD] = jnp.concatenate(rows, 0).astype(BF16)
        msg_ref[:, heads * HD :] = jnp.broadcast_to(gain_ref[...], (slots, chunk)).astype(BF16)

    return call(body, shaped((slots, heads * HD + chunk), BF16), [VM] * 3)(keep, came, gain_row)


def project(every, slot_row, weight, hidden, n_aux):
    depth, width = weight.shape
    requests, chunk = hidden.shape
    extra = every.shape[1] - depth

    def body(every_ref, slot_ref, w_ref, hid_ref, term_ref, msg_ref):
        place = lax.axis_index("head") * n_aux + lax.axis_index("aux")
        rows = every_ref[:, :depth].astype(F32)
        slot_col = to_column(slot_ref[...])
        sel = jnp.zeros((requests, depth), F32)
        for e in range(requests):
            sel = sel + jnp.where(slot_col == e, rows[e : e + 1, :], 0.0)
        term = jnp.dot(sel.astype(BF16), w_ref[...], preferred_element_type=F32)
        tiled = jnp.concatenate([hid_ref[...].astype(F32)] * (width // chunk), 1)
        owner = lax.broadcasted_iota(jnp.int32, term.shape, 1) // chunk == place
        term = term + jnp.where(owner, tiled, 0.0)
        term_ref[...] = term
        msg_ref[:, :width] = term.astype(BF16)
        msg_ref[:, width:] = every_ref[:, depth:]

    return call(
        body,
        (shaped((requests, width), F32), shaped((requests, width + extra), BF16)),
        [VM] * 4,
        grant=3 * MIB,
        cost=pl.CostEstimate(
            flops=2 * requests * weight.size, bytes_accessed=weight.size * 2, transcendentals=0
        ),
    )(every, slot_row, weight, hidden)


def add_terms(term, message, came, axis, step, last):
    requests, width = term.shape
    extra = message.shape[1] - width

    def body(term_ref, mine_ref, came_ref, *outs):
        upper = is_upper(axis, step)
        total = term_ref[...] + came_ref[:, :width].astype(F32)
        a, b = mine_ref[:, width:], came_ref[:, width:]
        low, high = jnp.where(upper, b, a), jnp.where(upper, a, b)
        if last:
            outs[0][...] = total.astype(BF16)
            outs[1][:, :extra] = low
            outs[1][:, extra:] = high
        else:
            outs[0][...] = total
            outs[1][:, :width] = total.astype(BF16)
            outs[1][:, width : width + extra] = low
            outs[1][:, width + extra :] = high

    if last:
        outs = (shaped((requests, width), BF16), shaped((requests, 2 * extra), BF16))
    else:
        outs = (shaped((requests, width), F32), shaped((requests, width + 2 * extra), BF16))
    return call(body, outs, [VM] * 3)(term, message, came)


def score(stream, gains, resident, lm_head):
    requests, depth = stream.shape
    width = lm_head.shape[1]
    block = gains.shape[1]
    held = len(resident)
    rows = depth // PIECES
    start = held * rows
    left = PIECES - held
    slots = min(3, left)
    stride = gains.shape[0] // (depth // block)

    def body(stream_ref, gain_ref, *refs):
        kept = refs[:held]
        src, out_ref, sum_ref, x_ref, buf, sem = refs[held:]

        def copy(i):
            return pltpu.make_async_copy(
                src.at[pl.ds(start + i * rows, rows)], buf.at[i % slots], sem.at[i % slots]
            )

        for i in range(slots):
            copy(i).start()
        squares = jnp.zeros((requests, 1), F32)
        for p in range(depth // block):
            part = stream_ref[:, p * block : (p + 1) * block].astype(F32)
            squares = squares + jnp.sum(part * part, axis=1, keepdims=True)
        factor = lax.rsqrt(squares / depth + 1e-05)
        for p in range(depth // block):
            part = stream_ref[:, p * block : (p + 1) * block].astype(F32)
            gain = gain_ref[p * stride : p * stride + 1, :].astype(F32)
            x_ref[:, p * block : (p + 1) * block] = (part * factor * gain).astype(BF16)

        def multiply(ref, piece, first=False):
            part = jnp.dot(
                x_ref[:, piece * rows : (piece + 1) * rows], ref[...], preferred_element_type=F32
            )
            out_ref[...] = part if first else out_ref[...] + part

        done = 0
        for i in range(held):
            multiply(kept[i], i, i == 0)
            while done < left and done * held < (i + 1) * left:
                copy(done).wait()
                multiply(buf.at[done % slots], held + done)
                if done + slots < left:
                    copy(done + slots).start()
                done += 1
        logits = out_ref[...]
        expd = jnp.exp(logits)
        total = jnp.sum(expd, axis=1, keepdims=True)
        moment = jnp.sum(expd * logits, axis=1, keepdims=True)
        lane = lax.broadcasted_iota(jnp.int32, (requests, 128), 1)
        sum_ref[...] = jnp.where(lane == 0, total, moment)

    return call(
        body,
        (shaped((requests, width), F32), shaped((requests, 128), F32)),
        [VM] * (2 + held) + [HB],
        [
            pltpu.VMEM((requests, depth), BF16),
            pltpu.VMEM((slots, rows, width), BF16),
            pltpu.SemaphoreType.DMA((slots,)),
        ],
        slots * rows * width * 2 + 4 * MIB,
        pl.CostEstimate(
            flops=2 * requests * lm_head.size,
            bytes_accessed=left * rows * width * 2,
            transcendentals=requests * width,
        ),
    )(stream, gains, *resident, lm_head)


def make_per_device(sizes):
    n_pool, n_head, n_aux = sizes["pool"], sizes["head"], sizes["aux"]

    def per_device(
        hidden,
        gain,
        queries,
        new_key,
        new_value,
        cache_key,
        cache_value,
        lengths,
        slot_of,
        out_proj,
        lm_head,
    ):
        rounds = Rounds(lm_head)
        slot_row, length_row = slot_of.reshape(1, -1), lengths.reshape(1, -1)

        every = gather(rounds, join(queries, new_key, new_value), "pool", n_pool, 0)

        widths = (queries.shape[1], new_key.shape[1])
        halves = steps_of(n_head)[::-1]
        keep, message = attend(
            every, slot_row, length_row, cache_key, cache_value, widths, halves[0]
        )
        for i, step in enumerate(halves):
            came = rounds.swap(message, "head", n_head, step)
            if i + 1 < len(halves):
                keep, message = split_again(keep, came, halves[i + 1])
        message = finish(keep, came, gain.reshape(1, -1))
        every = gather(rounds, message, "pool", n_pool, 0)

        term, message = project(every, slot_row, out_proj[0], hidden, n_aux)
        todo = [("aux", n_aux, s) for s in steps_of(n_aux)]
        todo += [("head", n_head, s) for s in steps_of(n_head)]
        for i, (axis, size, step) in enumerate(todo):
            came = rounds.swap(message, axis, size, step)
            term, message = add_terms(term, message, came, axis, step, i + 1 == len(todo))

        stream = gather(rounds, term, "pool", n_pool, 1)
        logits, sums = score(stream, message, rounds.resident, lm_head)
        for axis, size in (("aux", n_aux), ("head", n_head), ("pool", n_pool)):
            for step in steps_of(size):
                sums = sums + rounds.swap(sums, axis, size, step)
        entropy = jnp.log(sums[:, 0]) - sums[:, 1] / sums[:, 0]
        return (logits, entropy)

    return per_device


def solution(mesh):
    in_specs = (
        P("grp", ("pool", "head", "aux")),
        P(("pool", "head", "aux")),
        P(("grp", "pool"), "aux"),
        P(("grp", "pool"), "aux"),
        P(("grp", "pool"), "aux"),
        P(("grp", "pool"), "head", "aux"),
        P(("grp", "pool"), "head", "aux"),
        P("grp"),
        P("grp"),
        P("aux", "head", "pool"),
        P(None, ("pool", "head", "aux")),
    )
    out_specs = (P("grp", ("pool", "head", "aux")), P("grp"))
    return jax.shard_map(
        make_per_device(dict(mesh.shape)),
        mesh=mesh,
        in_specs=in_specs,
        out_specs=out_specs,
        check_vma=False,
    )
```

time: 126 us -> 94.1 us (0.75)
  local copies, waits for them, and re-layouts: 40 us -> 10.9 us
  other arithmetic: 6.18 us -> 0.71 us
  waiting for transfers between devices: 21 us -> 24.4 us
  matrix products: 2.42 us -> 0 us
  Pallas kernels: 31.2 us -> 33.6 us
    unnamed x62 -> x22, local copies, waits for them, and re-layouts: 39.8 us -> 10.9 us
    convert_element_type x8 -> x0, other arithmetic: 3.04 us -> none  [the longest x1 0.78 us: per_device(): stream = term.astype(bf16)]
    dot_general x3 -> x0, matrix products: 2.42 us -> none  [the longest x1 1.22 us: per_device(): jnp.einsum('skgt,stkd->skgd', weights.astype(bf16), values, preferred_ele...]
    pallas_call x11 -> x21, Pallas kernels: 31.2 us -> 33.6 us  [the longest x8 17.7 us: fetch(): call(body, pltpu.VMEM((rows, lm_head.shape[1]), lm_head.dtype), [HB], [pl...]
    ppermute x8, waiting for transfers between devices: 11.5 us -> 13.6 us  [swap(): y = lax.ppermute(x, axis, pairs)]
    ppermute x5, starting transfers between devices: 4.75 us -> 3.44 us  [swap(): return lax.ppermute(x, axis, pairs)]
    ppermute x5, waiting for transfers between devices: 9.45 us -> 10.7 us  [swap(): return lax.ppermute(x, axis, pairs)]
  transfers between devices with their start and end apart: 13 -> 13, of which waited for: 12 -> 12; matrix products, arithmetic and copies ran while one was open for 2% -> 0% of each run, Pallas kernels for 14% -> 19%
where the time goes in v1:
time: 94.1 us; the launch traced here: 93.5 us
  Pallas kernels  33.6 us (36%)
  waiting for transfers between devices  24.4 us (26%)
  starting transfers between devices  23.2 us (25%)
  local copies, waits for them, and re-layouts  10.9 us (12%)
    ppermute x8, starting transfers between devices, swap(): y = lax.ppermute(x, axis, pairs)  19.8 us
    pallas_call x8, Pallas kernels, fetch(): call(body, pltpu.VMEM((rows, lm_head.shape[1]), lm_head.dtype), [HB], [pl...  17.7 us
    ppermute x8, waiting for transfers between devices, swap(): y = lax.ppermute(x, axis, pairs)  13.6 us
    pallas_call x1, Pallas kernels, score(): call(body, (shaped((requests, width), F32), shaped((requests, 128), F32))...  12.2 us
    unnamed x22, local copies, waits for them, and re-layouts  10.9 us
    ppermute x5, waiting for transfers between devices, swap(): return lax.ppermute(x, axis, pairs)  10.7 us
    ppermute x5, starting transfers between devices, swap(): return lax.ppermute(x, axis, pairs)  3.44 us
  transfers between devices with their start and end apart: 13, of which 12 were waited for; matrix products, arithmetic and copies ran while one was open for 0% of the time, Pallas kernels for 19%

profile of v1, /device:TPU:0, one launch (start us, length us, event | category | flops | bytes accessed | tf_op | source)
XLA Modules:
  0.0 93.5 jit_solution(795090130041027338)
XLA Ops:
  0.6 0.7 copy-done.3
  1.4 0.7 copy-done.7
  2.0 0.7 copy-done.8
  2.8 3.1 %collective-permute-start = (bf16[2,5120]{1,0:T(2,128)(2,1)S(1)}, bf16[2,5120]{1,0:T(2,128)(2,1)S(1)}, u32[]{:S(2)}, u32[]{:S(2)}) collective-permute-start(bf16[2,5120]{1,0:T(2,128)(2,1)S(1)} %shard_map.122.x_ref), channel_id=1, source_target_pairs={{0,4},{4,0},{8,12},{12,8},{1,5},{5,1},{9,13},{13,9},{2,6},{6,2},{1... | collective-permute-start | bytes 61448 | tf_op jit(solution)/shard_map/ppermute | solution.py:75
  5.9 1.8 %collective-permute-done.y_ref = bf16[2,5120]{1,0:T(2,128)(2,1)S(1)} collective-permute-done((bf16[2,5120]{1,0:T(2,128)(2,1)S(1)}, bf16[2,5120]{1,0:T(2,128)(2,1)S(1)}, u32[]{:S(2)}, u32[]{:S(2)}) %collective-permute-start) | collective-permute-done | bytes 20512 | tf_op jit(solution)/shard_map/ppermute | solution.py:75
  7.7 3.1 %collective-permute-start.1 = (bf16[4,5120]{1,0:T(4,128)(2,1)S(1)}, bf16[4,5120]{1,0:T(4,128)(2,1)S(1)}, u32[]{:S(2)}, u32[]{:S(2)}) collective-permute-start(bf16[4,5120]{1,0:T(4,128)(2,1)S(1)} %shard_map.123.x_ref), channel_id=1, source_target_pairs={{0,8},{4,12},{8,0},{12,4},{1,9},{5,13},{9,1},{13,5},{2,10},{6,14},... | collective-permute-start | bytes 122888 | tf_op jit(solution)/shard_map/ppermute | solution.py:75
  10.8 2.0 %collective-permute-done.1.y_ref = bf16[4,5120]{1,0:T(4,128)(2,1)S(1)} collective-permute-done((bf16[4,5120]{1,0:T(4,128)(2,1)S(1)}, bf16[4,5120]{1,0:T(4,128)(2,1)S(1)}, u32[]{:S(2)}, u32[]{:S(2)}) %collective-permute-start.1) | collective-permute-done | bytes 40992 | tf_op jit(solution)/shard_map/ppermute | solution.py:75
  12.8 1.0 %copy-done.1 = bf16[2,256,512]{2,1,0:T(8,128)(2,1)S(1)} copy-done((bf16[2,256,512]{2,1,0:T(8,128)(2,1)S(1)}, bf16[2,256,512]{2,1,0:T(8,128)(2,1)}, u32[]{:S(2)}) %copy-start.1) | copy-done | bytes 524312
  13.8 1.0 %copy-done.2 = bf16[2,256,512]{2,1,0:T(8,128)(2,1)S(1)} copy-done((bf16[2,256,512]{2,1,0:T(8,128)(2,1)S(1)}, bf16[2,256,512]{2,1,0:T(8,128)(2,1)}, u32[]{:S(2)}) %copy-start.2) | copy-done | bytes 524312
  14.9 0.7 copy-done.5
  15.5 0.7 copy-done.10
  16.2 0.7 shard_map.125
  16.9 1.9 %collective-permute-start.2 = (bf16[2,16,384]{2,1,0:T(8,128)(2,1)S(1)}, bf16[2,16,384]{2,1,0:T(8,128)(2,1)S(1)}, u32[]{:S(2)}, u32[]{:S(2)}) collective-permute-start(bf16[2,16,384]{2,1,0:T(8,128)(2,1)S(1)} %get-tuple-element.13), channel_id=1, source_target_pairs={{0,2},{2,0},{1,3},{3,1},{4,6},{6,4},{5,7},{7,5},{8,10},{10,8},{9,1... | collective-permute-start | bytes 73736 | tf_op jit(solution)/shard_map/ppermute | solution.py:75
  18.8 2.0 %collective-permute-done.2.came_ref = bf16[2,16,384]{2,1,0:T(8,128)(2,1)S(1)} collective-permute-done((bf16[2,16,384]{2,1,0:T(8,128)(2,1)S(1)}, bf16[2,16,384]{2,1,0:T(8,128)(2,1)S(1)}, u32[]{:S(2)}, u32[]{:S(2)}) %collective-permute-start.2) | collective-permute-done | bytes 24608 | tf_op jit(solution)/shard_map/ppermute | solution.py:75
  20.8 0.7 copy-done.9
  21.5 2.0 %collective-permute-start.3 = (bf16[2,2560]{1,0:T(2,128)(2,1)S(1)}, bf16[2,2560]{1,0:T(2,128)(2,1)S(1)}, u32[]{:S(2)}, u32[]{:S(2)}) collective-permute-start(bf16[2,2560]{1,0:T(2,128)(2,1)S(1)} %shard_map.126.x_ref), channel_id=1, source_target_pairs={{0,4},{4,0},{8,12},{12,8},{1,5},{5,1},{9,13},{13,9},{2,6},{6,2},{1... | collective-permute-start | bytes 30728 | tf_op jit(solution)/shard_map/ppermute | solution.py:75
  23.5 1.8 %collective-permute-done.3.y_ref = bf16[2,2560]{1,0:T(2,128)(2,1)S(1)} collective-permute-done((bf16[2,2560]{1,0:T(2,128)(2,1)S(1)}, bf16[2,2560]{1,0:T(2,128)(2,1)S(1)}, u32[]{:S(2)}, u32[]{:S(2)}) %collective-permute-start.3) | collective-permute-done | bytes 10272 | tf_op jit(solution)/shard_map/ppermute | solution.py:75
  25.3 3.0 %collective-permute-start.4 = (bf16[4,2560]{1,0:T(4,128)(2,1)S(1)}, bf16[4,2560]{1,0:T(4,128)(2,1)S(1)}, u32[]{:S(2)}, u32[]{:S(2)}) collective-permute-start(bf16[4,2560]{1,0:T(4,128)(2,1)S(1)} %shard_map.127.x_ref), channel_id=1, source_target_pairs={{0,8},{4,12},{8,0},{12,4},{1,9},{5,13},{9,1},{13,5},{2,10},{6,14},... | collective-permute-start | bytes 61448 | tf_op jit(solution)/shard_map/ppermute | solution.py:75
  28.3 1.8 %collective-permute-done.4.y_ref = bf16[4,2560]{1,0:T(4,128)(2,1)S(1)} collective-permute-done((bf16[4,2560]{1,0:T(4,128)(2,1)S(1)}, bf16[4,2560]{1,0:T(4,128)(2,1)S(1)}, u32[]{:S(2)}, u32[]{:S(2)}) %collective-permute-start.4) | collective-permute-done | bytes 20512 | tf_op jit(solution)/shard_map/ppermute | solution.py:75
  30.1 3.4 %copy-done = bf16[1,2048,2048]{2,1,0:T(8,128)(2,1)S(1)} copy-done((bf16[1,2048,2048]{2,1,0:T(8,128)(2,1)S(1)}, bf16[1,2048,2048]{2,1,0:T(8,128)(2,1)}, u32[]{:S(2)}) %copy-start) | copy-done | bytes 8388632
  33.4 0.7 copy-done.4
  34.1 0.7 copy-done.6
  34.8 1.3 %shard_map.129 = (f32[8,2048]{1,0:T(8,128)S(1)}, bf16[8,2560]{1,0:T(8,128)(2,1)S(1)}) custom-call(bf16[8,2560]{1,0:T(8,128)(2,1)S(1)} %shard_map.128.every_ref, s32[1,8]{1,0:T(1,128)S(1)} %bitcast.6, bf16[2048,2048]{1,0:T(8,128)(2,1)S(1)} %bitcast.4, bf16[8,512]{1,0:T(8,128)(2,1)S(1)} %copy-done.4), custom_call_target="tpu_custom_call" | custom-call | flops 67108864 | bytes 8388608 | tf_op jit(solution)/shard_map/pallas_call | solution.py:279
  36.1 1.2 %collective-permute-done.5.came_ref = bf16[8,2560]{1,0:T(8,128)(2,1)S(1)} collective-permute-done((bf16[8,2560]{1,0:T(8,128)(2,1)S(1)}, bf16[8,2560]{1,0:T(8,128)(2,1)S(1)}, u32[]{:S(2)}, u32[]{:S(2)}) %collective-permute-start.5) | collective-permute-done | bytes 40992 | tf_op jit(solution)/shard_map/ppermute | solution.py:73
  37.3 1.9 %collective-permute-start.6 = (bf16[8,3072]{1,0:T(8,128)(2,1)S(1)}, bf16[8,3072]{1,0:T(8,128)(2,1)S(1)}, u32[]{:S(2)}, u32[]{:S(2)}) collective-permute-start(bf16[8,3072]{1,0:T(8,128)(2,1)S(1)} %get-tuple-element.17.mine_ref), channel_id=1, source_target_pairs={{0,2},{2,0},{1,3},{3,1},{4,6},{6,4},{5,7},{7,5},{8,10},{10,8},{9,1... | collective-permute-start | bytes 147464 | tf_op jit(solution)/shard_map/ppermute | solution.py:75
  39.2 2.3 %collective-permute-done.6.came_ref = bf16[8,3072]{1,0:T(8,128)(2,1)S(1)} collective-permute-done((bf16[8,3072]{1,0:T(8,128)(2,1)S(1)}, bf16[8,3072]{1,0:T(8,128)(2,1)S(1)}, u32[]{:S(2)}, u32[]{:S(2)}) %collective-permute-start.6) | collective-permute-done | bytes 49184 | tf_op jit(solution)/shard_map/ppermute | solution.py:75
  41.5 1.9 %collective-permute-start.7 = (bf16[8,2048]{1,0:T(8,128)(2,1)S(1)}, bf16[8,2048]{1,0:T(8,128)(2,1)S(1)}, u32[]{:S(2)}, u32[]{:S(2)}) collective-permute-start(bf16[8,2048]{1,0:T(8,128)(2,1)S(1)} %get-tuple-element.18.x_ref), channel_id=1, source_target_pairs={{0,4},{4,0},{8,12},{12,8},{1,5},{5,1},{9,13},{13,9},{2,6},{6,2},{1... | collective-permute-start | bytes 98312 | tf_op jit(solution)/shard_map/ppermute | solution.py:75
  43.4 2.0 %collective-permute-done.7.y_ref = bf16[8,2048]{1,0:T(8,128)(2,1)S(1)} collective-permute-done((bf16[8,2048]{1,0:T(8,128)(2,1)S(1)}, bf16[8,2048]{1,0:T(8,128)(2,1)S(1)}, u32[]{:S(2)}, u32[]{:S(2)}) %collective-permute-start.7) | collective-permute-done | bytes 32800 | tf_op jit(solution)/shard_map/ppermute | solution.py:75
  45.5 0.6 shard_map.132.x_ref
  46.1 2.9 %collective-permute-start.8 = (bf16[8,4096]{1,0:T(8,128)(2,1)}, bf16[8,4096]{1,0:T(8,128)(2,1)}, u32[]{:S(2)}, u32[]{:S(2)}) collective-permute-start(bf16[8,4096]{1,0:T(8,128)(2,1)} %shard_map.132.x_ref), channel_id=1, source_target_pairs={{0,8},{4,12},{8,0},{12,4},{1,9},{5,13},{9,1},{13,5},{2,10},{6,14},... | collective-permute-start | bytes 196616 | tf_op jit(solution)/shard_map/ppermute | solution.py:75
  49.0 2.2 %shard_map.140.refs_6_ = bf16[512,4096]{1,0:T(8,128)(2,1)S(1)} custom-call(bf16[8192,4096]{1,0:T(8,128)(2,1)} %refs_8_.1), custom_call_target="tpu_custom_call" | custom-call | bytes 4194304 | tf_op jit(solution)/shard_map/pallas_call | solution.py:55
  51.2 2.2 %shard_map.139.refs_5_ = bf16[512,4096]{1,0:T(8,128)(2,1)S(1)} custom-call(bf16[8192,4096]{1,0:T(8,128)(2,1)} %refs_8_.1), custom_call_target="tpu_custom_call" | custom-call | bytes 4194304 | tf_op jit(solution)/shard_map/pallas_call | solution.py:55
  53.4 2.2 %shard_map.138.refs_4_ = bf16[512,4096]{1,0:T(8,128)(2,1)S(1)} custom-call(bf16[8192,4096]{1,0:T(8,128)(2,1)} %refs_8_.1), custom_call_target="tpu_custom_call" | custom-call | bytes 4194304 | tf_op jit(solution)/shard_map/pallas_call | solution.py:55
  55.7 2.2 %shard_map.137.refs_3_ = bf16[512,4096]{1,0:T(8,128)(2,1)S(1)} custom-call(bf16[8192,4096]{1,0:T(8,128)(2,1)} %refs_8_.1), custom_call_target="tpu_custom_call" | custom-call | bytes 4194304 | tf_op jit(solution)/shard_map/pallas_call | solution.py:55
  57.9 2.2 %shard_map.136.refs_2_ = bf16[512,4096]{1,0:T(8,128)(2,1)S(1)} custom-call(bf16[8192,4096]{1,0:T(8,128)(2,1)} %refs_8_.1), custom_call_target="tpu_custom_call" | custom-call | bytes 4194304 | tf_op jit(solution)/shard_map/pallas_call | solution.py:55
  60.1 2.2 %shard_map.135.refs_1_ = bf16[512,4096]{1,0:T(8,128)(2,1)S(1)} custom-call(bf16[8192,4096]{1,0:T(8,128)(2,1)} %refs_8_.1), custom_call_target="tpu_custom_call" | custom-call | bytes 4194304 | tf_op jit(solution)/shard_map/pallas_call | solution.py:55
  62.3 2.2 %shard_map.134.refs_0_ = bf16[512,4096]{1,0:T(8,128)(2,1)S(1)} custom-call(bf16[8192,4096]{1,0:T(8,128)(2,1)} %refs_8_.1), custom_call_target="tpu_custom_call" | custom-call | bytes 4194304 | tf_op jit(solution)/shard_map/pallas_call | solution.py:55
  64.5 2.2 %shard_map.141.refs_7_ = bf16[512,4096]{1,0:T(8,128)(2,1)S(1)} custom-call(bf16[8192,4096]{1,0:T(8,128)(2,1)} %refs_8_.1), custom_call_target="tpu_custom_call" | custom-call | bytes 4194304 | tf_op jit(solution)/shard_map/pallas_call | solution.py:55
  66.8 0.9 shard_map.133.stream_ref
  67.7 12.2 %shard_map.142 = (f32[8,4096]{1,0:T(8,128)}, f32[8,128]{1,0:T(8,128)S(1)}) custom-call(bf16[8,8192]{1,0:T(8,128)(2,1)S(1)} %shard_map.133.stream_ref, bf16[8,2048]{1,0:T(8,128)(2,1)S(1)} %get-tuple-element.19.gain_ref, bf16[512,4096]{1,0:T(8,128)(2,1)S(1)} %shard_map.134.refs_0_, bf16[512,4096]{1,0:T(8,128)(2,1)S(1)} %shard_map.135.refs_1_, ...), custom_call_target="tpu_custom_call" | custom-call | flops 536870912 | bytes 33554432 | tf_op jit(solution)/shard_map/pallas_call | solution.py:370
  79.9 0.1 collective-permute-start.9
  80.0 1.2 %collective-permute-done.9 = f32[8,128]{1,0:T(8,128)S(1)} collective-permute-done((f32[8,128]{1,0:T(8,128)S(1)}, f32[8,128]{1,0:T(8,128)S(1)}, u32[]{:S(2)}, u32[]{:S(2)}) %collective-permute-start.9) | collective-permute-done | bytes 4128 | tf_op jit(solution)/shard_map/ppermute | solution.py:73
  81.1 1.5 %collective-permute-start.10 = (f32[8,128]{1,0:T(8,128)S(1)}, f32[8,128]{1,0:T(8,128)S(1)}, u32[]{:S(2)}, u32[]{:S(2)}) collective-permute-start(f32[8,128]{1,0:T(8,128)S(1)} %add.12), channel_id=1, source_target_pairs={{0,2},{2,0},{1,3},{3,1},{4,6},{6,4},{5,7},{7,5},{8,10},{10,8},{9,1... | collective-permute-start | bytes 12296 | tf_op jit(solution)/shard_map/ppermute | solution.py:73
  82.6 2.1 %collective-permute-done.10 = f32[8,128]{1,0:T(8,128)S(1)} collective-permute-done((f32[8,128]{1,0:T(8,128)S(1)}, f32[8,128]{1,0:T(8,128)S(1)}, u32[]{:S(2)}, u32[]{:S(2)}) %collective-permute-start.10) | collective-permute-done | bytes 4128 | tf_op jit(solution)/shard_map/ppermute | solution.py:73
  84.7 1.9 %collective-permute-start.11 = (f32[8,128]{1,0:T(8,128)S(1)}, f32[8,128]{1,0:T(8,128)S(1)}, u32[]{:S(2)}, u32[]{:S(2)}) collective-permute-start(f32[8,128]{1,0:T(8,128)S(1)} %add.13), channel_id=1, source_target_pairs={{0,4},{4,0},{8,12},{12,8},{1,5},{5,1},{9,13},{13,9},{2,6},{6,2},{1... | collective-permute-start | bytes 12296 | tf_op jit(solution)/shard_map/ppermute | solution.py:73
  86.6 1.7 %collective-permute-done.11 = f32[8,128]{1,0:T(8,128)S(1)} collective-permute-done((f32[8,128]{1,0:T(8,128)S(1)}, f32[8,128]{1,0:T(8,128)S(1)}, u32[]{:S(2)}, u32[]{:S(2)}) %collective-permute-start.11) | collective-permute-done | bytes 4128 | tf_op jit(solution)/shard_map/ppermute | solution.py:73
  88.3 4.5 %collective-permute-done.12 = f32[8,128]{1,0:T(8,128)S(1)} collective-permute-done((f32[8,128]{1,0:T(8,128)S(1)}, f32[8,128]{1,0:T(8,128)S(1)}, u32[]{:S(2)}, u32[]{:S(2)}) %collective-permute-start.12) | collective-permute-done | bytes 4128 | tf_op jit(solution)/shard_map/ppermute | solution.py:73
  92.8 0.7 subtract_reduce_fusion
  (26 shorter events, 0.2 us)
Async XLA Ops:
  0.6 0.7 copy-start.3
  1.3 0.7 copy-start.7
  2.0 0.7 copy-start.8
  2.8 4.9 %collective-permute-start = (bf16[2,5120]{1,0:T(2,128)(2,1)S(1)}, bf16[2,5120]{1,0:T(2,128)(2,1)S(1)}, u32[]{:S(2)}, u32[]{:S(2)}) collective-permute-start(bf16[2,5120]{1,0:T(2,128)(2,1)S(1)} %shard_map.122.x_ref), channel_id=1, source_target_pairs={{0,4},{4,0},{8,12},{12,8},{1,5},{5,1},{9,13},{13,9},{2,6},{6,2},{1... | collective-permute-start | bytes 61448 | tf_op jit(solution)/shard_map/ppermute | solution.py:75
  7.7 5.1 %collective-permute-start.1 = (bf16[4,5120]{1,0:T(4,128)(2,1)S(1)}, bf16[4,5120]{1,0:T(4,128)(2,1)S(1)}, u32[]{:S(2)}, u32[]{:S(2)}) collective-permute-start(bf16[4,5120]{1,0:T(4,128)(2,1)S(1)} %shard_map.123.x_ref), channel_id=1, source_target_pairs={{0,8},{4,12},{8,0},{12,4},{1,9},{5,13},{9,1},{13,5},{2,10},{6,14},... | collective-permute-start | bytes 122888 | tf_op jit(solution)/shard_map/ppermute | solution.py:75
  12.8 1.0 %copy-start.1 = (bf16[2,256,512]{2,1,0:T(8,128)(2,1)S(1)}, bf16[2,256,512]{2,1,0:T(8,128)(2,1)}, u32[]{:S(2)}) copy-start(bf16[2,256,512]{2,1,0:T(8,128)(2,1)} %key_ref.1) | copy-start | bytes 1572868
  13.8 1.0 %copy-start.2 = (bf16[2,256,512]{2,1,0:T(8,128)(2,1)S(1)}, bf16[2,256,512]{2,1,0:T(8,128)(2,1)}, u32[]{:S(2)}) copy-start(bf16[2,256,512]{2,1,0:T(8,128)(2,1)} %value_ref.1) | copy-start | bytes 1572868
  14.9 0.7 copy-start.5
  15.5 0.7 copy-start.10
  16.9 3.9 %collective-permute-start.2 = (bf16[2,16,384]{2,1,0:T(8,128)(2,1)S(1)}, bf16[2,16,384]{2,1,0:T(8,128)(2,1)S(1)}, u32[]{:S(2)}, u32[]{:S(2)}) collective-permute-start(bf16[2,16,384]{2,1,0:T(8,128)(2,1)S(1)} %get-tuple-element.13), channel_id=1, source_target_pairs={{0,2},{2,0},{1,3},{3,1},{4,6},{6,4},{5,7},{7,5},{8,10},{10,8},{9,1... | collective-permute-start | bytes 73736 | tf_op jit(solution)/shard_map/ppermute | solution.py:75
  20.8 0.7 copy-start.9
  21.5 3.7 %collective-permute-start.3 = (bf16[2,2560]{1,0:T(2,128)(2,1)S(1)}, bf16[2,2560]{1,0:T(2,128)(2,1)S(1)}, u32[]{:S(2)}, u32[]{:S(2)}) collective-permute-start(bf16[2,2560]{1,0:T(2,128)(2,1)S(1)} %shard_map.126.x_ref), channel_id=1, source_target_pairs={{0,4},{4,0},{8,12},{12,8},{1,5},{5,1},{9,13},{13,9},{2,6},{6,2},{1... | collective-permute-start | bytes 30728 | tf_op jit(solution)/shard_map/ppermute | solution.py:75
  25.3 4.8 %collective-permute-start.4 = (bf16[4,2560]{1,0:T(4,128)(2,1)S(1)}, bf16[4,2560]{1,0:T(4,128)(2,1)S(1)}, u32[]{:S(2)}, u32[]{:S(2)}) collective-permute-start(bf16[4,2560]{1,0:T(4,128)(2,1)S(1)} %shard_map.127.x_ref), channel_id=1, source_target_pairs={{0,8},{4,12},{8,0},{12,4},{1,9},{5,13},{9,1},{13,5},{2,10},{6,14},... | collective-permute-start | bytes 61448 | tf_op jit(solution)/shard_map/ppermute | solution.py:75
  30.1 3.4 %copy-start = (bf16[1,2048,2048]{2,1,0:T(8,128)(2,1)S(1)}, bf16[1,2048,2048]{2,1,0:T(8,128)(2,1)}, u32[]{:S(2)}) copy-start(bf16[1,2048,2048]{2,1,0:T(8,128)(2,1)} %param.20) | copy-start | bytes 25165828
  33.4 0.7 copy-start.4
  34.1 0.7 copy-start.6
  36.1 1.2 %collective-permute-start.5 = (bf16[8,2560]{1,0:T(8,128)(2,1)S(1)}, bf16[8,2560]{1,0:T(8,128)(2,1)S(1)}, u32[]{:S(2)}, u32[]{:S(2)}) collective-permute-start(bf16[8,2560]{1,0:T(8,128)(2,1)S(1)} %get-tuple-element.15.mine_ref), channel_id=1, source_target_pairs={{0,1},{1,0},{2,3},{3,2},{4,5},{5,4},{6,7},{7,6},{8,9},{9,8},{10,11... | collective-permute-start | bytes 122888 | tf_op jit(solution)/shard_map/ppermute | solution.py:73
  37.3 4.2 %collective-permute-start.6 = (bf16[8,3072]{1,0:T(8,128)(2,1)S(1)}, bf16[8,3072]{1,0:T(8,128)(2,1)S(1)}, u32[]{:S(2)}, u32[]{:S(2)}) collective-permute-start(bf16[8,3072]{1,0:T(8,128)(2,1)S(1)} %get-tuple-element.17.mine_ref), channel_id=1, source_target_pairs={{0,2},{2,0},{1,3},{3,1},{4,6},{6,4},{5,7},{7,5},{8,10},{10,8},{9,1... | collective-permute-start | bytes 147464 | tf_op jit(solution)/shard_map/ppermute | solution.py:75
  41.5 4.0 %collective-permute-start.7 = (bf16[8,2048]{1,0:T(8,128)(2,1)S(1)}, bf16[8,2048]{1,0:T(8,128)(2,1)S(1)}, u32[]{:S(2)}, u32[]{:S(2)}) collective-permute-start(bf16[8,2048]{1,0:T(8,128)(2,1)S(1)} %get-tuple-element.18.x_ref), channel_id=1, source_target_pairs={{0,4},{4,0},{8,12},{12,8},{1,5},{5,1},{9,13},{13,9},{2,6},{6,2},{1... | collective-permute-start | bytes 98312 | tf_op jit(solution)/shard_map/ppermute | solution.py:75
  46.1 20.7 %collective-permute-start.8 = (bf16[8,4096]{1,0:T(8,128)(2,1)}, bf16[8,4096]{1,0:T(8,128)(2,1)}, u32[]{:S(2)}, u32[]{:S(2)}) collective-permute-start(bf16[8,4096]{1,0:T(8,128)(2,1)} %shard_map.132.x_ref), channel_id=1, source_target_pairs={{0,8},{4,12},{8,0},{12,4},{1,9},{5,13},{9,1},{13,5},{2,10},{6,14},... | collective-permute-start | bytes 196616 | tf_op jit(solution)/shard_map/ppermute | solution.py:75
  79.9 1.2 %collective-permute-start.9 = (f32[8,128]{1,0:T(8,128)S(1)}, f32[8,128]{1,0:T(8,128)S(1)}, u32[]{:S(2)}, u32[]{:S(2)}) collective-permute-start(f32[8,128]{1,0:T(8,128)S(1)} %get-tuple-element.21), channel_id=1, source_target_pairs={{0,1},{1,0},{2,3},{3,2},{4,5},{5,4},{6,7},{7,6},{8,9},{9,8},{10,11... | collective-permute-start | bytes 12296 | tf_op jit(solution)/shard_map/ppermute | solution.py:73
  81.1 3.6 %collective-permute-start.10 = (f32[8,128]{1,0:T(8,128)S(1)}, f32[8,128]{1,0:T(8,128)S(1)}, u32[]{:S(2)}, u32[]{:S(2)}) collective-permute-start(f32[8,128]{1,0:T(8,128)S(1)} %add.12), channel_id=1, source_target_pairs={{0,2},{2,0},{1,3},{3,1},{4,6},{6,4},{5,7},{7,5},{8,10},{10,8},{9,1... | collective-permute-start | bytes 12296 | tf_op jit(solution)/shard_map/ppermute | solution.py:73
  84.7 3.6 %collective-permute-start.11 = (f32[8,128]{1,0:T(8,128)S(1)}, f32[8,128]{1,0:T(8,128)S(1)}, u32[]{:S(2)}, u32[]{:S(2)}) collective-permute-start(f32[8,128]{1,0:T(8,128)S(1)} %add.13), channel_id=1, source_target_pairs={{0,4},{4,0},{8,12},{12,8},{1,5},{5,1},{9,13},{13,9},{2,6},{6,2},{1... | collective-permute-start | bytes 12296 | tf_op jit(solution)/shard_map/ppermute | solution.py:73
  88.3 4.5 %collective-permute-start.12 = (f32[8,128]{1,0:T(8,128)S(1)}, f32[8,128]{1,0:T(8,128)S(1)}, u32[]{:S(2)}, u32[]{:S(2)}) collective-permute-start(f32[8,128]{1,0:T(8,128)S(1)} %add.14), channel_id=1, source_target_pairs={{0,8},{4,12},{8,0},{12,4},{1,9},{5,13},{9,1},{13,5},{2,10},{6,14},... | collective-permute-start | bytes 12296 | tf_op jit(solution)/shard_map/ppermute | solution.py:73
